TPU v7x, 32 devices: a whole 2x2x4 slice. The times are simulated.
32 devices in a mesh: group: 4 (over y, core), slab: 8 (over z, x).
Axes of the slice: x: 2, y: 2, z: 4, core: 2. Of those that a mesh axis runs over, the one named last changes fastest.
Arguments:
- state: float32 [8, 64, 32, 256], P('group', 'slab'), may hold values from -3 to 3
- theta: float32 [8, 32, 16, 128], P('group', 'slab'), may hold values from -2.5 to 2.5
- forcing: float32 [64, 32, 256], P('slab'), may hold values from -6 to 6
- boxes: int32 [6, 4096], replicated, may hold values from 0 to 64, as said below
- observed: float32 [4096], P('slab'), may hold values from -6 to 6
- noise_var: float32 [4096], P('slab'), may hold values from 0.05 to 0.5
- perturb: float32 [8, 4096], P('group', 'slab'), may hold values from -6 to 6
Outputs:
- final_state: float32 [8, 64, 32, 256], P('group', 'slab')
- theta_new: float32 [8, 32, 16, 128], P('group', 'slab')
Inputs may be any that keep to these rules, and one draw needn't show every extreme that they name: `boxes`: for every observation z0 < z1 <= 64, y0 < y1 <= 8, x0 < x1 <= 64; a box spans at most 16 planes, 4 tiles along the second dimension and 8 along the third (fewer where the grid is narrower), and these most are reached.
All inputs are finite; a program needn't handle non-finite values.
Results may differ from a plain program's by a relative error of at most 0.00019.
Values sent between devices are 32-bit elements; how exact they have to be, the bound alone decides.
A program may use at most 64 MiB of HBM per device.

v0:
```python
import jax
import jax.numpy as jnp
from jax import lax
from jax.sharding import PartitionSpec as P

STEP_SIZE = 0.1


def extended(cells, sides, width):
    for axis, dim in sides:
        count = lax.axis_size(axis)
        ends = count - 1
        head = lax.slice_in_dim(cells, 0, width, axis=dim)
        tail = lax.slice_in_dim(cells, cells.shape[dim] - width, cells.shape[dim], axis=dim)
        cells = jnp.concatenate(
            [
                lax.ppermute(tail, axis, [(i, (i + 1) % count) for i in range(ends)]),
                cells,
                lax.ppermute(head, axis, [((i + 1) % count, i) for i in range(ends)]),
            ],
            axis=dim,
        )
    return cells


def advance(padded, diffusivity, forcing):
    center = padded[:, 1:-1]
    side_pad = jnp.pad(center, ((0, 0), (0, 0), (1, 1), (1, 1)))
    beside_all = padded[:, 2:] + padded[:, :-2]
    beside_all = beside_all + side_pad[:, :, 2:, 1:-1] + side_pad[:, :, :-2, 1:-1]
    beside_all = beside_all + side_pad[:, :, 1:-1, 2:] + side_pad[:, :, 1:-1, :-2]
    change = (
        diffusivity * (beside_all - 6.0 * center) + 0.5 * center * (1.0 - center * center) + forcing
    )
    return center + STEP_SIZE * change


def upsample(params):
    return jnp.repeat(jnp.repeat(jnp.repeat(params, 2, axis=1), 2, axis=2), 2, axis=3)


def local(state, theta, forcing, boxes, observed, noise_var, perturb):
    mem_local, planes, rows_y, rows_x = state.shape
    slab_index = lax.axis_index("slab")
    diffusivity = 0.5 * jnp.exp(upsample(theta))
    current = state
    for sweep in range(2):
        padded = extended(current, (("slab", 1),), 1)
        current = advance(padded, diffusivity, forcing[None])
    tiles_y = rows_y // 4
    tiles_x = rows_x // 4
    tiles = current.reshape(mem_local, planes, tiles_y, 4, tiles_x, 4).sum(axis=(3, 5))
    tile_rows = tiles.reshape(mem_local * planes * tiles_y, tiles_x)
    obs_total = boxes.shape[1]
    width = 2048
    box_blocks = jnp.moveaxis(boxes.reshape(6, obs_total // width, width), 1, 0)
    plane_global = slab_index * planes + jnp.arange(planes, dtype=jnp.int32)
    index_y = jnp.arange(tiles_y, dtype=jnp.int32)
    index_x = jnp.arange(tiles_x, dtype=jnp.int32)

    def observe(block):
        in_x = ((index_x[:, None] >= block[4][None]) & (index_x[:, None] < block[5][None])).astype(
            jnp.float32
        )
        in_y = ((index_y[:, None] >= block[2][None]) & (index_y[:, None] < block[3][None])).astype(
            jnp.float32
        )
        in_z = (
            (plane_global[:, None] >= block[0][None]) & (plane_global[:, None] < block[1][None])
        ).astype(jnp.float32)
        count = ((block[1] - block[0]) * (block[3] - block[2]) * (block[5] - block[4]) * 16).astype(
            jnp.float32
        )
        along_x = jnp.dot(tile_rows, in_x, precision=lax.Precision.HIGHEST)
        along_x = along_x.reshape(mem_local, planes, tiles_y, width)
        weight = in_z[:, None, :] * in_y[None, :, :] / count[None, None, :]
        return jnp.sum(along_x * weight[None], axis=(1, 2))

    partial_value = lax.map(observe, box_blocks)
    partial_value = jnp.moveaxis(partial_value, 0, 1).reshape(mem_local, obs_total)
    pred_share = lax.psum_scatter(partial_value, "slab", scatter_dimension=1, tiled=True)
    predicted, perturbs = (
        lax.all_gather(pred_share, "group", axis=0, tiled=True),
        lax.all_gather(perturb, "group", axis=0, tiled=True),
    )
    members = predicted.shape[0]
    scale = jnp.sqrt(jnp.float32(members - 1))
    anomaly = (predicted - jnp.mean(predicted, axis=0, keepdims=True)) / scale
    misfit = observed[None] + jnp.sqrt(noise_var)[None] * perturbs - predicted
    weighted = anomaly / noise_var[None]
    inner_part = jnp.dot(weighted, anomaly.T, precision=lax.Precision.HIGHEST)
    cross_part = jnp.dot(weighted, misfit.T, precision=lax.Precision.HIGHEST)
    inner, cross = lax.psum((inner_part, cross_part), "slab")
    identity = jnp.eye(members, dtype=jnp.float32)
    factor = jnp.linalg.cholesky(identity + inner)
    gain = jax.scipy.linalg.cho_solve((factor, True), cross)
    mixing = identity + (gain - jnp.mean(gain, axis=0, keepdims=True)) / scale
    flat_theta = theta.reshape(mem_local, -1)
    everyone = lax.all_gather(flat_theta, "group", axis=0, tiled=True)
    columns = lax.dynamic_slice_in_dim(mixing, lax.axis_index("group") * mem_local, mem_local, 1)
    updated = jnp.dot(columns.T, everyone, precision=lax.Precision.HIGHEST)
    return (current, updated.reshape(theta.shape))


def solution(mesh):
    return jax.shard_map(
        local,
        mesh=mesh,
        in_specs=(
            P("group", "slab", None, None),
            P("group", "slab", None, None),
            P("slab", None, None),
            P(),
            P("slab"),
            P("slab"),
            P("group", "slab"),
        ),
        out_specs=(P("group", "slab", None, None), P("group", "slab", None, None)),
        check_vma=False,
    )
```

profile of v0, /device:TPU:0, one launch (start us, length us, event | category | flops | bytes accessed | tf_op | source)
XLA Modules:
  0.0 157.5 jit_solution(17179000041874202507)
XLA Ops:
  7.2 1.5 fusion.60
  8.7 1.3 collective-permute-start
  10.0 6.1 %collective-permute-start.1 = (f32[2,1,32,256]{3,2,1,0:T(8,128)}, f32[2,1,32,256]{3,2,1,0:T(8,128)}, u32[]{:S(2)}, u32[]{:S(2)}) collective-permute-start(f32[2,1,32,256]{3,2,1,0:T(8,128)} %get-tuple-element.116), channel_id=1, source_target_pairs={{0,1},{1,2},{2,3},{3,4},{4,5},{5,6},{6,7},{8,9},{9,10},{10,11},{11... | collective-permute-start | bytes 196616 | tf_op jit(solution)/shard_map/ppermute | solution.py:17
  16.2 0.9 exponential_multiply_fusion
  17.1 0.4 copy.128
  17.7 0.6 copy.129
  18.4 0.2 copy-done.1
  18.8 1.3 fusion.22
  20.1 1.3 collective-permute-start.2
  21.4 4.8 %collective-permute-start.3 = (f32[2,1,32,256]{3,2,1,0:T(8,128)S(1)}, f32[2,1,32,256]{3,2,1,0:T(8,128)S(1)}, u32[]{:S(2)}, u32[]{:S(2)}) collective-permute-start(f32[2,1,32,256]{3,2,1,0:T(8,128)S(1)} %get-tuple-element.114), channel_id=1, source_target_pairs={{0,1},{1,2},{2,3},{3,4},{4,5},{5,6},{6,7},{8,9},{9,10},{10,11},{11... | collective-permute-start | bytes 196616 | tf_op jit(solution)/shard_map/ppermute | solution.py:17
  26.3 5.2 %all-gather.1 = f32[4,2,512]{2,1,0:T(2,128)S(1)} all-gather(f32[1,2,512]{2,1,0:T(2,128)S(1)} %bitcast.90), channel_id=1, replica_groups=mesh['group'=4,'slab'=8] {'group'}, dimensions={0}, use_global_device_ids=true | all-gather | bytes 20480 | tf_op jit(solution)/shard_map/all_gather | solution.py:84
  31.6 0.4 fusion.32
  32.1 4.6 %copy.131 = f32[2,8,32,256]{1,3,2,0:T(8,128)} copy(f32[2,8,32,256]{3,2,1,0:T(8,128)S(1)} %fusion.32) | data formatting | bytes 1048576 | tf_op jit(solution)/shard_map/add | solution.py:35
  36.7 6.1 %reduce_sum.36 = f32[2,8,8,64]{1,3,2,0:T(8,128)S(1)} reduce(f32[2,8,8,4,64,4]{1,5,4,3,2,0:T(4,128)} %bitcast.72, f32[]{:T(128)} %constant.83.clone.1), dimensions={3,5}, to_apply=%region_0.1 | reduce | flops 122880 | bytes 557060 | tf_op jit(solution)/shard_map/reduce_sum | solution.py:52
  43.0 4.0 %while.12 = (s32[]{:T(128)}, f32[2,2,2048]{2,1,0:T(2,128)S(1)}, s32[2,6,2048]{2,1,0:T(8,128)}, f32[128,64]{1,0:T(8,128)S(1)}, s32[]{:T(128)}, /*index=5*/s32[]{:...) while((s32[]{:T(128)}, f32[2,2,2048]{2,1,0:T(2,128)S(1)}, ...), condition=%wide.region_3.4_spmd.clone.clone, body=%wide.region_1.3_spmd.clone.clone.sunk | while | flops 202647568 | bytes 1556753 | solution.py:79
  43.0 1.1 multiply_convert_fusion.2
  44.3 0.6 multiply_reduce_fusion.2
  45.0 1.1 multiply_convert_fusion.2
  46.3 0.6 multiply_reduce_fusion.2
  47.0 2.0 %copy.140 = f32[2,4096]{0,1:T(8,128)} copy(f32[2,4096]{1,0:T(2,128)S(1)} %bitcast.88) | data formatting | bytes 65536
  49.0 6.0 %all-gather.2 = f32[4,2,8192]{2,1,0:T(2,128)S(1)} all-gather(f32[1,2,8192]{2,1,0:T(2,128)S(1)} %reshape.202), channel_id=1, replica_groups=mesh['group'=4,'slab'=8] {'group'}, dimensions={0}, use_global_device_ids=true | all-gather | bytes 327680 | tf_op jit(solution)/shard_map/all_gather | solution.py:99
  55.2 64.8 %reduce-scatter.4.cloned.1.call-done = f32[512,2]{1,0:T(8,128)} async-done(((f32[4096,2]{1,0:T(8,128)}), f32[512,2]{1,0:T(8,128)}) %reduce-scatter.4.cloned.1.call-update) | async-done | bytes 4112
  120.0 1.1 copy.141
  121.1 5.2 %all-gather = f32[4,2,512]{2,1,0:T(2,128)S(1)} all-gather(f32[1,2,512]{2,1,0:T(2,128)S(1)} %bitcast.89), channel_id=1, replica_groups=mesh['group'=4,'slab'=8] {'group'}, dimensions={0}, use_global_device_ids=true | all-gather | bytes 20480 | tf_op jit(solution)/shard_map/all_gather | solution.py:83
  126.7 19.4 %all-reduce.2 = (f32[8,8]{1,0:T(8,128)S(1)}, f32[8,8]{0,1:T(8,128)S(1)}) all-reduce(f32[8,8]{1,0:T(8,128)S(1)} %fusion.35, f32[8,8]{0,1:T(8,128)S(1)} %fusion.40), channel_id=1, replica_groups=mesh['group'=4,'slab'=8] {'slab'}, use_global_device_ids=true, to_apply=%region_9.10 | all-reduce | flops 128 | bytes 1024 | tf_op jit(solution)/shard_map/psum | solution.py:93
  146.1 0.7 cholesky.14
  147.0 0.6 compare_reduce_fusion
  147.7 0.6 select_select_fusion
  148.4 0.6 custom-call.10
  149.2 0.3 fusion.61
  149.6 0.4 convolution_bitcast_fusion
  150.0 0.6 copy.142
  (52 shorter events, 2.2 us)
Async XLA Ops:
  7.2 112.9 %reduce-scatter.4.cloned.1.call-start = ((), (), s32[]{:S(2)}) async-start(), calls=%async_computation.1 | async-start | bytes 2359296
  8.7 9.7 %collective-permute-start = (f32[2,1,32,256]{3,2,1,0:T(8,128)}, f32[2,1,32,256]{3,2,1,0:T(8,128)S(1)}, u32[]{:S(2)}, u32[]{:S(2)}) collective-permute-start(f32[2,1,32,256]{3,2,1,0:T(8,128)} %get-tuple-element.115), channel_id=1, source_target_pairs={{1,0},{2,1},{3,2},{4,3},{5,4},{6,5},{7,6},{9,8},{10,9},{11,10},{12... | collective-permute-start | bytes 196616 | tf_op jit(solution)/shard_map/ppermute | solution.py:19
  10.0 8.4 %collective-permute-start.1 = (f32[2,1,32,256]{3,2,1,0:T(8,128)}, f32[2,1,32,256]{3,2,1,0:T(8,128)}, u32[]{:S(2)}, u32[]{:S(2)}) collective-permute-start(f32[2,1,32,256]{3,2,1,0:T(8,128)} %get-tuple-element.116), channel_id=1, source_target_pairs={{0,1},{1,2},{2,3},{3,4},{4,5},{5,6},{6,7},{8,9},{9,10},{10,11},{11... | collective-permute-start | bytes 196616 | tf_op jit(solution)/shard_map/ppermute | solution.py:17
  17.7 1.0 copy-start.1
  17.7 1.1 copy-start.2
  17.7 8.6 %copy-start.3 = (f32[2,4,16,128]{3,2,1,0:T(8,128)S(1)}, f32[2,4,16,128]{3,2,1,0:T(8,128)}, u32[]{:S(2)}) copy-start(f32[2,4,16,128]{3,2,1,0:T(8,128)} %param.10) | copy-start | bytes 196612
  17.7 8.6 %copy-start.4 = (f32[2,512]{1,0:T(2,128)S(1)}, f32[2,512]{1,0:T(2,128)}, u32[]{:S(2)}) copy-start(f32[2,512]{1,0:T(2,128)} %param.15) | copy-start | bytes 12292
  17.7 13.8 %copy-start.5 = (f32[512]{0:T(512)S(1)}, f32[512]{0:T(512)}, u32[]{:S(2)}) copy-start(f32[512]{0:T(512)} %param.14) | copy-start | bytes 6148
  20.1 11.5 %collective-permute-start.2 = (f32[2,1,32,256]{3,2,1,0:T(8,128)S(1)}, f32[2,1,32,256]{3,2,1,0:T(8,128)S(1)}, u32[]{:S(2)}, u32[]{:S(2)}) collective-permute-start(f32[2,1,32,256]{3,2,1,0:T(8,128)S(1)} %get-tuple-element.113), channel_id=1, source_target_pairs={{1,0},{2,1},{3,2},{4,3},{5,4},{6,5},{7,6},{9,8},{10,9},{11,10},{12... | collective-permute-start | bytes 196616 | tf_op jit(solution)/shard_map/ppermute | solution.py:19
  21.4 10.2 %collective-permute-start.3 = (f32[2,1,32,256]{3,2,1,0:T(8,128)S(1)}, f32[2,1,32,256]{3,2,1,0:T(8,128)S(1)}, u32[]{:S(2)}, u32[]{:S(2)}) collective-permute-start(f32[2,1,32,256]{3,2,1,0:T(8,128)S(1)} %get-tuple-element.114), channel_id=1, source_target_pairs={{0,1},{1,2},{2,3},{3,4},{4,5},{5,6},{6,7},{8,9},{9,10},{10,11},{11... | collective-permute-start | bytes 196616 | tf_op jit(solution)/shard_map/ppermute | solution.py:17
  32.0 4.6 %copy-start = (f32[2,8,32,256]{3,2,1,0:T(8,128)}, f32[2,8,32,256]{3,2,1,0:T(8,128)S(1)}, u32[]{:S(2)}) copy-start(f32[2,8,32,256]{3,2,1,0:T(8,128)S(1)} %fusion.32) | copy-start | bytes 1572868
  49.0 77.5 %copy-start.6 = (f32[512]{0:T(512)S(1)}, f32[512]{0:T(512)}, u32[]{:S(2)}) copy-start(f32[512]{0:T(512)} %param.13) | copy-start | bytes 6148
Sparse Core Ops, SparseCore 0:
  49.1 70.8 reduce-scatter.3
where the time goes:
time: 158 us; the launch traced here: 157 us
  waiting for transfers between devices  64.9 us (41%)
  blocking collectives  35.8 us (23%)
  between operations  14.3 us (9%)
  other arithmetic  14.2 us (9%)
  starting transfers between devices  13.6 us (9%)
  local copies, waits for them, and re-layouts  12.3 us (8%)
  matrix products  2.47 us (2%)
    unnamed x2, waiting for transfers between devices  64.9 us
    psum x1, blocking collectives, local(): inner, cross = lax.psum((inner_part, cross_part), 'slab')  19.4 us
    ppermute x2, starting transfers between devices, extended(): lax.ppermute(tail, axis, [(i, (i + 1) % count) for i in range(ends)])  11 us
    reduce_sum x1, other arithmetic, local(): current.reshape(mem_local, planes, tiles_y, 4, tiles_x, 4).sum(axis=(3, 5))  6.15 us
    all_gather x1, blocking collectives, local(): everyone = lax.all_gather(flat_theta, 'group', axis=0, tiled=True)  6.01 us
    all_gather x1, blocking collectives, local(): lax.all_gather(perturb, 'group', axis=0, tiled=True)  5.21 us
    all_gather x1, blocking collectives, local(): lax.all_gather(pred_share, 'group', axis=0, tiled=True)  5.2 us
    add x1, local copies, waits for them, and re-layouts, advance(): return center + STEP_SIZE * change  4.61 us
  transfers between devices with their start and end apart: 5, of which 1 were waited for; matrix products, arithmetic and copies ran while one was open for 2% of the time, Pallas kernels for 0%

commit v1 on v0

v1 whole, which is shorter than its diff:
```python
import functools
import math

import jax
import jax.numpy as jnp
from jax import lax
from jax.experimental import pallas as pl
from jax.experimental.pallas import tpu as pltpu
from jax.sharding import PartitionSpec as P

STEP_SIZE = 0.1
LANES = 128
TILE = 4
MESH = pl.DeviceIdType.MESH
HIGHEST = lax.Precision.HIGHEST


def remote(src, dst, send, recv, device):
    return pltpu.make_async_remote_copy(
        src_ref=src, dst_ref=dst, send_sem=send, recv_sem=recv, device_id=device, device_id_type=MESH
    )


def drain(ref, sem):
    pltpu.make_async_copy(ref, ref, sem).wait()


def split_dot(left, right):
    return jnp.dot(left, right, precision=HIGHEST, preferred_element_type=jnp.float32)


def kernel(
    groups, slabs, sub,
    state_ref, theta_ref, forcing_ref, boxes_ref, observed_ref, noise_ref, perturb_ref,
    final_ref, theta_new_ref,
    mid, diff, halo, maskx, halves, tile_rows, part_send, part_recv, pert_all, theta_all, sums_send, sums_recv,
    halo_send, halo_recv, theta_send_sem, theta_recv_sem, pert_send_sem, pert_recv_sem,
    part_send_sem, part_recv_sem, sums_send_sem, sums_recv_sem,
):
    mem, planes, rows, cols = state_ref.shape
    coarse_z, coarse_y, coarse_x = theta_ref.shape[1:]
    tiles_y = rows // TILE
    members = groups * mem
    total = groups * slabs
    obs_total = boxes_ref.shape[1]
    obs_slab = obs_total // slabs
    g = lax.axis_index("group")
    s = lax.axis_index("slab")
    me = s * groups + g

    barrier = pltpu.get_barrier_semaphore()

    def greet(step, carry):
        other = lax.rem(me + step, total)
        pl.semaphore_signal(
            barrier, inc=1, device_id=(lax.rem(other, groups), other // groups), device_id_type=MESH
        )
        return carry

    lax.fori_loop(1, total, greet, 0)

    lane = lax.broadcasted_iota(jnp.int32, (rows, cols), 1)
    row = lax.broadcasted_iota(jnp.int32, (rows, cols), 0)

    spread_x = (
        lax.broadcasted_iota(jnp.int32, (coarse_x, cols), 1) // 2
        == lax.broadcasted_iota(jnp.int32, (coarse_x, cols), 0)
    ).astype(jnp.float32)
    spread_y = (
        lax.broadcasted_iota(jnp.int32, (rows, coarse_y), 0) // 2
        == lax.broadcasted_iota(jnp.int32, (rows, coarse_y), 1)
    ).astype(jnp.float32)
    coarse = 0.5 * jnp.exp(theta_ref[...].reshape(mem * coarse_z * coarse_y, coarse_x))
    wide = split_dot(coarse, spread_x)
    for m in range(mem):
        for z in range(coarse_z):
            start = (m * coarse_z + z) * coarse_y
            diff[m, z] = split_dot(spread_y, wide[start : start + coarse_y])

    def step_plane(center, below, above, diffusivity, forcing):
        beside = below + above
        beside = beside + jnp.where(row == rows - 1, 0.0, pltpu.roll(center, rows - 1, 0))
        beside = beside + jnp.where(row == 0, 0.0, pltpu.roll(center, 1, 0))
        beside = beside + jnp.where(lane == cols - 1, 0.0, pltpu.roll(center, cols - 1, 1))
        beside = beside + jnp.where(lane == 0, 0.0, pltpu.roll(center, 1, 1))
        change = (
            diffusivity * (beside - 6.0 * center)
            + 0.5 * center * (1.0 - center * center)
            + forcing
        )
        return center + STEP_SIZE * change

    def inner_planes(src, dst):
        def body(z, carry):
            for m in range(mem):
                dst[m, z] = step_plane(
                    src[m, z], src[m, z - 1], src[m, z + 1], diff[m, z // 2], forcing_ref[z]
                )
            return carry

        lax.fori_loop(1, planes - 1, body, 0)

    def edge_plane(src, dst, sweep, side):
        z = 0 if side == 0 else planes - 1
        for m in range(mem):
            outer = halo[sweep, side, m]
            below = outer if side == 0 else src[m, z - 1]
            above = src[m, z + 1] if side == 0 else outer
            dst[m, z] = step_plane(src[m, z], below, above, diff[m, z // 2], forcing_ref[z])

    inner_planes(state_ref, mid)
    theta_all[g] = theta_ref[...]
    chunk = obs_slab // sub
    own = lax.rem(g, sub)
    own_cols = pl.ds(pl.multiple_of(own * chunk, LANES), chunk)
    pert_all[g] = perturb_ref[:, own_cols]

    pl.semaphore_wait(barrier, total - 1)

    def halo_copy(src, sweep, side):
        plane = 0 if side == 0 else planes - 1
        other = s - 1 if side == 0 else s + 1
        return remote(
            src.at[:, plane],
            halo.at[sweep, 1 - side],
            halo_send.at[sweep, side],
            halo_recv.at[sweep, 1 - side],
            (g, other),
        )

    def has(side):
        return s > 0 if side == 0 else s < slabs - 1

    def start_halo(src, sweep, side):
        @pl.when(has(side))
        def _():
            halo_copy(src, sweep, side).start()

    def wait_halo(sweep, side):
        @pl.when(has(side))
        def _():
            drain(halo.at[sweep, side], halo_recv.at[sweep, side])

        @pl.when(jnp.logical_not(has(side)))
        def _():
            halo[sweep, side] = jnp.zeros_like(halo[sweep, side])

    for side in range(2):
        start_halo(state_ref, 0, side)

    def share(step, carry):
        other = lax.rem(g + step, groups)
        want = lax.rem(other, sub)
        remote(
            perturb_ref.at[:, pl.ds(pl.multiple_of(want * chunk, LANES), chunk)],
            pert_all.at[g], pert_send_sem, pert_recv_sem, (other, s),
        ).start()
        remote(theta_ref, theta_all.at[g], theta_send_sem, theta_recv_sem, (other, s)).start()
        return carry

    lax.fori_loop(1, groups, share, 0)

    width = min(obs_slab, 512)
    tile_x = lax.broadcasted_iota(jnp.int32, (cols, width), 0) // TILE

    def build_mask(block, carry):
        at = pl.ds(pl.multiple_of(block * width, LANES), width)
        low = boxes_ref[4:5, at]
        high = boxes_ref[5:6, at]
        inside = jnp.where((tile_x >= low) & (tile_x < high), 1.0, 0.0)
        maskx[:, at] = inside.astype(jnp.bfloat16)
        return carry

    lax.fori_loop(0, obs_total // width, build_mask, 0)

    for side in range(2):
        wait_halo(0, side)
        edge_plane(state_ref, mid, 0, side)
        start_halo(mid, 1, side)
    inner_planes(mid, final_ref)
    for side in range(2):
        wait_halo(1, side)
        edge_plane(mid, final_ref, 1, side)

    small_lane = lax.broadcasted_iota(jnp.int32, (tiles_y, cols), 1) % TILE

    def collect(z, carry):
        for m in range(mem):
            for h in range(cols // LANES):
                halves[m, z, h] = final_ref[m, z, :, h * LANES : (h + 1) * LANES]
            parts = []
            for h in range(cols // LANES):
                part = halves[m, z, h, pl.ds(0, tiles_y, stride=TILE), :]
                for k in range(1, TILE):
                    part = part + halves[m, z, h, pl.ds(k, tiles_y, stride=TILE), :]
                parts.append(part)
            band = jnp.concatenate(parts, axis=1)
            band = band + pltpu.roll(band, 1, 1)
            band = band + pltpu.roll(band, 2, 1)
            high = band.astype(jnp.bfloat16).astype(jnp.float32)
            rest = band - high
            middle = rest.astype(jnp.bfloat16).astype(jnp.float32)
            low = rest - middle
            packed = jnp.where(
                small_lane == 3,
                high,
                jnp.where(
                    small_lane == 2,
                    pltpu.roll(middle, cols - 1, 1),
                    jnp.where(small_lane == 1, pltpu.roll(low, cols - 2, 1), 0.0),
                ),
            )
            tile_rows[m, z] = packed
        return carry

    lax.fori_loop(0, planes, collect, 0)
    left = tile_rows[...].reshape(mem * planes * tiles_y, cols).astype(jnp.bfloat16)
    tile_y = lax.broadcasted_iota(jnp.int32, (tiles_y, obs_slab), 0)

    def observe(step, carry):
        to = lax.rem(s + 1 + step, slabs)
        at = pl.ds(pl.multiple_of(to * obs_slab, LANES), obs_slab)
        along = jnp.dot(left, maskx[:, at], preferred_element_type=jnp.float32)
        box = boxes_ref[:, at]
        in_y = jnp.where((tile_y >= box[2:3]) & (tile_y < box[3:4]), 1.0, 0.0)
        sums = [jnp.zeros((tiles_y, obs_slab), jnp.float32) for _ in range(mem)]
        for z in range(planes):
            depth = s * planes + z
            in_z = jnp.where((depth >= box[0:1]) & (depth < box[1:2]), 1.0, 0.0)
            for m in range(mem):
                start = (m * planes + z) * tiles_y
                sums[m] = sums[m] + along[start : start + tiles_y] * in_z
        for m in range(mem):
            value = jnp.sum(sums[m] * in_y, axis=0, keepdims=True)
            for c in range(sub):
                part_send[to, c, m : m + 1, :] = value[:, c * chunk : (c + 1) * chunk]
        for k in range(groups):
            @pl.when(to * groups + k != me)
            def _():
                remote(
                    part_send.at[to, k % sub], part_recv.at[me], part_send_sem, part_recv_sem, (k, to)
                ).start()

        return carry

    lax.fori_loop(0, slabs, observe, 0)
    part_recv[me] = part_send[s, own]
    drain(part_recv.at[pl.ds(0, total - 1)], part_recv_sem)
    if groups > 1:
        drain(pert_all.at[pl.ds(0, groups - 1)], pert_recv_sem)

    pieces = []
    for k in range(groups):
        piece = part_recv[k]
        for t in range(1, slabs):
            piece = piece + part_recv[t * groups + k]
        pieces.append(piece)
    sums = jnp.concatenate(pieces, axis=0)
    perturbs = jnp.concatenate([pert_all[k] for k in range(groups)], axis=0)
    at = pl.ds(pl.multiple_of(s * obs_slab + own * chunk, LANES), chunk)
    box = boxes_ref[:, at]
    count = (box[1:2] - box[0:1]) * (box[3:4] - box[2:3]) * (box[5:6] - box[4:5]) * (TILE * TILE)
    predicted = sums / count.astype(jnp.float32)
    noise = noise_ref[:, own_cols]
    scale = math.sqrt(members - 1)
    anomaly = (predicted - jnp.mean(predicted, axis=0, keepdims=True)) / scale
    misfit = observed_ref[:, own_cols] + jnp.sqrt(noise) * perturbs - predicted
    weighted = anomaly / noise
    if sub != groups:
        weighted = weighted * (sub / groups)

    per_row = LANES // members
    packs = 2 * members // per_row
    small = (members, LANES)
    lane_m = lax.broadcasted_iota(jnp.int32, small, 1)
    row_m = lax.broadcasted_iota(jnp.int32, small, 0)
    for r in range(packs):
        packed = jnp.zeros(small, jnp.float32)
        for slot in range(per_row):
            j = r * per_row + slot
            other = anomaly[j : j + 1] if j < members else misfit[j - members : j - members + 1]
            value = jnp.sum(weighted * other, axis=1, keepdims=True)
            packed = packed + jnp.where(lane_m == slot * members + row_m, value, 0.0)
        sums_send[r : r + 1, :] = jnp.sum(packed, axis=0, keepdims=True)
    sums_recv[me] = sums_send[...]

    def spread(step, carry):
        other = lax.rem(me + step, total)
        remote(
            sums_send, sums_recv.at[me], sums_send_sem, sums_recv_sem,
            (lax.rem(other, groups), other // groups),
        ).start()
        return carry

    lax.fori_loop(1, total, spread, 0)
    drain(sums_recv.at[pl.ds(0, total - 1)], sums_recv_sem)
    if total <= 64:
        whole = sums_recv[0]
        for t in range(1, total):
            whole = whole + sums_recv[t]
    else:
        whole = lax.fori_loop(1, total, lambda t, c: c + sums_recv[t], sums_recv[0])

    system = jnp.where(lane_m == row_m, 1.0, 0.0)
    for j in range(2 * members):
        r, slot = j // per_row, j % per_row
        value = jnp.sum(
            jnp.where(lane_m == slot * members + row_m, whole[r : r + 1], 0.0), axis=1, keepdims=True
        )
        system = system + jnp.where(lane_m == j, value, 0.0)
    for k in range(members):
        pivot = system[k : k + 1] / system[k : k + 1, k : k + 1]
        system = jnp.where(row_m == k, pivot, system - system[:, k : k + 1] * pivot)
    mixing = (system - jnp.mean(system, axis=0, keepdims=True)) / scale
    mixing = mixing + jnp.where(lane_m == row_m + members, 1.0, 0.0)
    if groups > 1:
        drain(theta_all.at[pl.ds(0, groups - 1)], theta_recv_sem)
    for m in range(mem):
        column = jnp.sum(
            jnp.where(lane_m == members + g * mem + m, mixing, 0.0), axis=1, keepdims=True
        )
        column = jnp.broadcast_to(column, (members, coarse_x))
        fresh = jnp.zeros(theta_ref.shape[1:], jnp.float32)
        for k in range(members):
            fresh = fresh + theta_all[k // mem, k % mem] * column[k : k + 1][None]
        theta_new_ref[m] = fresh

    for sweep in range(2):
        for side in range(2):
            @pl.when(has(side))
            def _():
                drain(halo.at[sweep, side], halo_send.at[sweep, side])

    if groups > 1:
        drain(pert_all.at[pl.ds(0, groups - 1)], pert_send_sem)
        drain(theta_all.at[pl.ds(0, groups - 1)], theta_send_sem)
    drain(part_recv.at[pl.ds(0, total - 1)], part_send_sem)
    drain(sums_recv.at[pl.ds(0, total - 1)], sums_send_sem)


def local(groups, slabs, state, theta, forcing, boxes, observed, noise_var, perturb):
    mem, planes, rows, cols = state.shape
    total = groups * slabs
    obs_total = boxes.shape[1]
    obs_slab = obs_total // slabs
    sub = min(groups, obs_slab // LANES)
    chunk = obs_slab // sub
    members = groups * mem
    packs = 2 * members * members // LANES
    f32 = jnp.float32
    vmem = pl.BlockSpec(memory_space=pltpu.VMEM)
    dma = pltpu.SemaphoreType.DMA
    return pl.pallas_call(
        functools.partial(kernel, groups, slabs, sub),
        name="window",
        out_shape=(
            jax.ShapeDtypeStruct(state.shape, f32),
            jax.ShapeDtypeStruct(theta.shape, f32),
        ),
        in_specs=[vmem] * 7,
        out_specs=(vmem, vmem),
        scratch_shapes=[
            pltpu.VMEM(state.shape, f32),
            pltpu.VMEM((mem, theta.shape[1], rows, cols), f32),
            pltpu.VMEM((2, 2, mem, rows, cols), f32),
            pltpu.VMEM((cols, obs_total), jnp.bfloat16),
            pltpu.VMEM((mem, planes, cols // LANES, rows, LANES), f32),
            pltpu.VMEM((mem, planes, rows // TILE, cols), f32),
            pltpu.VMEM((slabs, sub, mem, chunk), f32),
            pltpu.VMEM((total, mem, chunk), f32),
            pltpu.VMEM((groups, mem, chunk), f32),
            pltpu.VMEM((groups,) + theta.shape, f32),
            pltpu.VMEM((packs, LANES), f32),
            pltpu.VMEM((total, packs, LANES), f32),
            dma((2, 2)), dma((2, 2)), dma, dma, dma, dma, dma, dma, dma, dma,
        ],
        compiler_params=pltpu.CompilerParams(collective_id=0, has_side_effects=True),
    )(state, theta, forcing, boxes, observed.reshape(1, -1), noise_var.reshape(1, -1), perturb)


def solution(mesh):
    return jax.shard_map(
        functools.partial(local, mesh.shape["group"], mesh.shape["slab"]),
        mesh=mesh,
        in_specs=(
            P("group", "slab", None, None),
            P("group", "slab", None, None),
            P("slab", None, None),
            P(),
            P("slab"),
            P("slab"),
            P("group", "slab"),
        ),
        out_specs=(P("group", "slab", None, None), P("group", "slab", None, None)),
        check_vma=False,
    )
```

time: 158 us -> 34.1 us (0.22)
  waiting for transfers between devices: 64.9 us -> 0 us
  blocking collectives: 35.8 us -> 0 us
  Pallas kernels: 0 us -> 30.8 us
  other arithmetic: 14.2 us -> 0 us
  between operations: 14.3 us -> 0.65 us
  starting transfers between devices: 13.6 us -> 0 us
  local copies, waits for them, and re-layouts: 12.3 us -> 2.55 us
  matrix products: 2.47 us -> 0 us
    unnamed x2 -> x0, waiting for transfers between devices: 64.9 us -> none
    pallas_call x0 -> x1, Pallas kernels: none -> 30.8 us  [local(): pl.pallas_call(functools.partial(kernel, groups, slabs, sub), name='windo...]
    psum x1 -> x0, blocking collectives: 19.4 us -> none  [local(): inner, cross = lax.psum((inner_part, cross_part), 'slab')]
    all_gather x3 -> x0, blocking collectives: 16.4 us -> none  [the longest x1 6.01 us: local(): everyone = lax.all_gather(flat_theta, 'group', axis=0, tiled=True)]
    ppermute x4 -> x0, starting transfers between devices: 13.5 us -> none  [the longest x2 11 us: extended(): lax.ppermute(tail, axis, [(i, (i + 1) % count) for i in range(ends)])]
    reduce_sum x2 -> x0, other arithmetic: 6.17 us -> none  [the longest x1 6.15 us: local(): current.reshape(mem_local, planes, tiles_y, 4, tiles_x, 4).sum(axis=(3, 5))]
    add x2 -> x0, local copies, waits for them, and re-layouts: 4.68 us -> none  [the longest x1 4.61 us: advance(): return center + STEP_SIZE * change]
    another operation x5 -> x0, other arithmetic: 2.76 us -> none  [the longest x3 1.49 us: local(): factor = jnp.linalg.cholesky(identity + inner)]
  transfers between devices with their start and end apart: 5 -> 0, of which waited for: 1 -> 0; matrix products, arithmetic and copies ran while one was open for 2% -> 0% of each run, Pallas kernels for 0% -> 0%
where the time goes in v1:
time: 34.1 us; the launch traced here: 34 us
  Pallas kernels  30.8 us (90%)
  local copies, waits for them, and re-layouts  2.55 us (7%)
  between operations  0.65 us (2%)
    pallas_call x1, Pallas kernels, local(): pl.pallas_call(functools.partial(kernel, groups, slabs, sub), name='windo...  30.8 us
    unnamed x4, local copies, waits for them, and re-layouts  2.55 us

profile of v1, /device:TPU:0, one launch (start us, length us, event | category | flops | bytes accessed | tf_op | source)
XLA Modules:
  0.0 34.0 jit_solution(11270355730763844748)
XLA Ops:
  0.6 30.8 %window.1 = (f32[2,8,32,256]{3,2,1,0:T(8,128)}, f32[2,4,16,128]{3,2,1,0:T(8,128)}) custom-call(f32[2,8,32,256]{3,2,1,0:T(8,128)} %state_ref.1, f32[2,4,16,128]{3,2,1,0:T(8,128)} %theta_ref.1, f32[8,32,256]{2,1,0:T(8,128)} %forcing_ref.1, s32[6,4096]{1,0:T(8,128)} %boxes_ref.1, f32[1,512]{1,0:T(1,128)} %bitcast.2, f32[1,512]{1,0:T(1,128)} %bitcast.3, ...), custom_call_target="tpu_custom_call" | custom-call | tf_op jit(solution)/shard_map/window/pallas_call | solution.py:353
  31.4 0.0 copy-start
  31.4 1.9 %copy.11 = f32[2,8,32,256]{3,2,1,0:T(8,128)} copy(f32[2,8,32,256]{3,2,1,0:T(8,128)} %get-tuple-element.4) | data formatting | bytes 1048576
  33.3 0.0 copy-done
  33.3 0.6 %copy.12 = f32[2,4,16,128]{3,2,1,0:T(8,128)} copy(f32[2,4,16,128]{3,2,1,0:T(8,128)S(1)} %copy-done) | data formatting | bytes 131072
Async XLA Ops:
  31.4 1.9 %copy-start = (f32[2,4,16,128]{3,2,1,0:T(8,128)S(1)}, f32[2,4,16,128]{3,2,1,0:T(8,128)}, u32[]{:S(2)}) copy-start(f32[2,4,16,128]{3,2,1,0:T(8,128)} %get-tuple-element.5) | copy-start | bytes 196612

commit v2 on v1

--- a/solution.py
+++ b/solution.py
@@ -31,33 +31,86 @@
 
 def kernel(
     groups, slabs, sub,
-    state_ref, theta_ref, forcing_ref, boxes_ref, observed_ref, noise_ref, perturb_ref,
+    state_hbm, theta_hbm, forcing_hbm, boxes_hbm, observed_hbm, noise_hbm, perturb_hbm,
     final_ref, theta_new_ref,
-    mid, diff, halo, maskx, halves, tile_rows, part_send, part_recv, pert_all, theta_all, sums_send, sums_recv,
-    halo_send, halo_recv, theta_send_sem, theta_recv_sem, pert_send_sem, pert_recv_sem,
+    state_ref, forcing_ref, boxes_ref, observed_ref, noise_ref,
+    mid, diff, halo, maskx, halves, tile_rows, part_sum,
+    part_send, part_recv, pert_all, theta_all, sums_send, sums_recv,
+    load_sem, halo_send, halo_recv, theta_send_sem, theta_recv_sem, pert_send_sem, pert_recv_sem,
     part_send_sem, part_recv_sem, sums_send_sem, sums_recv_sem,
 ):
     mem, planes, rows, cols = state_ref.shape
-    coarse_z, coarse_y, coarse_x = theta_ref.shape[1:]
+    coarse_z, coarse_y, coarse_x = theta_hbm.shape[1:]
     tiles_y = rows // TILE
     members = groups * mem
     total = groups * slabs
     obs_total = boxes_ref.shape[1]
     obs_slab = obs_total // slabs
+    chunk = obs_slab // sub
     g = lax.axis_index("group")
     s = lax.axis_index("slab")
     me = s * groups + g
+    own = lax.rem(g, sub)
+    own_cols = pl.ds(pl.multiple_of(own * chunk, LANES), chunk)
+
+    def wrap(value, size):
+        return jnp.where(value >= size, value - size, value)
+
+    def each_slab(body):
+        if total <= 64:
+            for i in range(slabs):
+                half = (i + 1) // 2
+                rel = (slabs // 2 + (half if i % 2 == 0 else -half)) % slabs
+                body(wrap(s + rel, slabs), rel == 0)
+        else:
+
+            def loop(i, carry):
+                half = lax.div(i + 1, 2)
+                rel = slabs // 2 + jnp.where(lax.rem(i, 2) == 0, half, -half)
+                body(lax.rem(s + rel, slabs), None)
+                return carry
+
+            lax.fori_loop(0, slabs, loop, 0)
+
+    def each_peer(to, here, send):
+        if here is None:
+            for k in range(groups):
+                @pl.when((to != s) | (g != k))
+                def _():
+                    send(k)
+        elif here:
+            for step in range(1, groups):
+                send(wrap(g + step, groups))
+        else:
+            for k in range(groups):
+                send(k)
 
     barrier = pltpu.get_barrier_semaphore()
 
-    def greet(step, carry):
-        other = lax.rem(me + step, total)
-        pl.semaphore_signal(
-            barrier, inc=1, device_id=(lax.rem(other, groups), other // groups), device_id_type=MESH
-        )
-        return carry
-
-    lax.fori_loop(1, total, greet, 0)
+    def greet(to, here):
+        each_peer(
+            to, here,
+            lambda k: pl.semaphore_signal(barrier, inc=1, device_id=(k, to), device_id_type=MESH),
+        )
+
+    each_slab(greet)
+
+    loads = [
+        pltpu.make_async_copy(src, dst, load_sem.at[i])
+        for i, (src, dst) in enumerate(
+            (
+                (theta_hbm, theta_all.at[g]),
+                (state_hbm, state_ref),
+                (forcing_hbm, forcing_ref),
+                (boxes_hbm, boxes_ref),
+                (perturb_hbm.at[:, own_cols], pert_all.at[g]),
+                (observed_hbm, observed_ref),
+                (noise_hbm, noise_ref),
+            )
+        )
+    ]
+    for load in loads:
+        load.start()
 
     lane = lax.broadcasted_iota(jnp.int32, (rows, cols), 1)
     row = lax.broadcasted_iota(jnp.int32, (rows, cols), 0)
@@ -70,7 +123,8 @@
         lax.broadcasted_iota(jnp.int32, (rows, coarse_y), 0) // 2
         == lax.broadcasted_iota(jnp.int32, (rows, coarse_y), 1)
     ).astype(jnp.float32)
-    coarse = 0.5 * jnp.exp(theta_ref[...].reshape(mem * coarse_z * coarse_y, coarse_x))
+    loads[0].wait()
+    coarse = 0.5 * jnp.exp(theta_all[g].reshape(mem * coarse_z * coarse_y, coarse_x))
     wide = split_dot(coarse, spread_x)
     for m in range(mem):
         for z in range(coarse_z):
@@ -108,12 +162,9 @@
             above = src[m, z + 1] if side == 0 else outer
             dst[m, z] = step_plane(src[m, z], below, above, diff[m, z // 2], forcing_ref[z])
 
+    loads[1].wait()
+    loads[2].wait()
     inner_planes(state_ref, mid)
-    theta_all[g] = theta_ref[...]
-    chunk = obs_slab // sub
-    own = lax.rem(g, sub)
-    own_cols = pl.ds(pl.multiple_of(own * chunk, LANES), chunk)
-    pert_all[g] = perturb_ref[:, own_cols]
 
     pl.semaphore_wait(barrier, total - 1)
 
@@ -146,45 +197,40 @@
             halo[sweep, side] = jnp.zeros_like(halo[sweep, side])
 
     for side in range(2):
-        start_halo(state_ref, 0, side)
-
-    def share(step, carry):
-        other = lax.rem(g + step, groups)
+        start_halo(state_hbm, 0, side)
+
+    for step in range(1, groups):
+        other = wrap(g + step, groups)
         want = lax.rem(other, sub)
         remote(
-            perturb_ref.at[:, pl.ds(pl.multiple_of(want * chunk, LANES), chunk)],
+            perturb_hbm.at[:, pl.ds(pl.multiple_of(want * chunk, LANES), chunk)],
             pert_all.at[g], pert_send_sem, pert_recv_sem, (other, s),
         ).start()
-        remote(theta_ref, theta_all.at[g], theta_send_sem, theta_recv_sem, (other, s)).start()
-        return carry
-
-    lax.fori_loop(1, groups, share, 0)
-
-    width = min(obs_slab, 512)
-    tile_x = lax.broadcasted_iota(jnp.int32, (cols, width), 0) // TILE
+        remote(theta_hbm, theta_all.at[g], theta_send_sem, theta_recv_sem, (other, s)).start()
+
+    for load in loads[3:]:
+        load.wait()
+    tile_x = lax.broadcasted_iota(jnp.int32, (cols, obs_slab), 0) // TILE
 
     def build_mask(block, carry):
-        at = pl.ds(pl.multiple_of(block * width, LANES), width)
+        at = pl.ds(pl.multiple_of(block * obs_slab, LANES), obs_slab)
         low = boxes_ref[4:5, at]
         high = boxes_ref[5:6, at]
         inside = jnp.where((tile_x >= low) & (tile_x < high), 1.0, 0.0)
         maskx[:, at] = inside.astype(jnp.bfloat16)
         return carry
 
-    lax.fori_loop(0, obs_total // width, build_mask, 0)
+    lax.fori_loop(0, slabs, build_mask, 0)
 
     for side in range(2):
         wait_halo(0, side)
         edge_plane(state_ref, mid, 0, side)
         start_halo(mid, 1, side)
     inner_planes(mid, final_ref)
-    for side in range(2):
-        wait_halo(1, side)
-        edge_plane(mid, final_ref, 1, side)
 
     small_lane = lax.broadcasted_iota(jnp.int32, (tiles_y, cols), 1) % TILE
 
-    def collect(z, carry):
+    def collect(z):
         for m in range(mem):
             for h in range(cols // LANES):
                 halves[m, z, h] = final_ref[m, z, :, h * LANES : (h + 1) * LANES]
@@ -201,7 +247,7 @@
             rest = band - high
             middle = rest.astype(jnp.bfloat16).astype(jnp.float32)
             low = rest - middle
-            packed = jnp.where(
+            tile_rows[z, m] = jnp.where(
                 small_lane == 3,
                 high,
                 jnp.where(
@@ -210,40 +256,64 @@
                     jnp.where(small_lane == 1, pltpu.roll(low, cols - 2, 1), 0.0),
                 ),
             )
-            tile_rows[m, z] = packed
+
+    def weigh(left, at, zs, sums):
+        along = jnp.dot(left, maskx[:, at], preferred_element_type=jnp.float32)
+        low = boxes_ref[0:1, at]
+        high = boxes_ref[1:2, at]
+        for i, z in enumerate(zs):
+            depth = s * planes + z
+            in_z = jnp.where((depth >= low) & (depth < high), 1.0, 0.0)
+            for m in range(mem):
+                start = (i * mem + m) * tiles_y
+                term = along[start : start + tiles_y] * in_z
+                sums[m] = term if sums[m] is None else sums[m] + term
+        return sums
+
+    def collect_inner(z, carry):
+        collect(z)
         return carry
 
-    lax.fori_loop(0, planes, collect, 0)
-    left = tile_rows[...].reshape(mem * planes * tiles_y, cols).astype(jnp.bfloat16)
+    lax.fori_loop(1, planes - 1, collect_inner, 0)
+    inner_rows = tile_rows[1 : planes - 1].reshape((planes - 2) * mem * tiles_y, cols)
+    inner_rows = inner_rows.astype(jnp.bfloat16)
+
+    def observe_inner(block, carry):
+        at = pl.ds(pl.multiple_of(block * obs_slab, LANES), obs_slab)
+        sums = weigh(inner_rows, at, range(1, planes - 1), [None] * mem)
+        for m in range(mem):
+            part_sum[m, :, at] = sums[m]
+        return carry
+
+    lax.fori_loop(0, slabs, observe_inner, 0, unroll=2)
+
+    for side in range(2):
+        wait_halo(1, side)
+        edge_plane(mid, final_ref, 1, side)
+        collect(0 if side == 0 else planes - 1)
+    edge_rows = jnp.concatenate(
+        [tile_rows[z].reshape(mem * tiles_y, cols) for z in (0, planes - 1)], axis=0
+    ).astype(jnp.bfloat16)
     tile_y = lax.broadcasted_iota(jnp.int32, (tiles_y, obs_slab), 0)
 
-    def observe(step, carry):
-        to = lax.rem(s + 1 + step, slabs)
+    def observe(to, here):
         at = pl.ds(pl.multiple_of(to * obs_slab, LANES), obs_slab)
-        along = jnp.dot(left, maskx[:, at], preferred_element_type=jnp.float32)
-        box = boxes_ref[:, at]
-        in_y = jnp.where((tile_y >= box[2:3]) & (tile_y < box[3:4]), 1.0, 0.0)
-        sums = [jnp.zeros((tiles_y, obs_slab), jnp.float32) for _ in range(mem)]
-        for z in range(planes):
-            depth = s * planes + z
-            in_z = jnp.where((depth >= box[0:1]) & (depth < box[1:2]), 1.0, 0.0)
-            for m in range(mem):
-                start = (m * planes + z) * tiles_y
-                sums[m] = sums[m] + along[start : start + tiles_y] * in_z
+        sums = weigh(edge_rows, at, (0, planes - 1), [part_sum[m, :, at] for m in range(mem)])
+        in_y = jnp.where((tile_y >= boxes_ref[2:3, at]) & (tile_y < boxes_ref[3:4, at]), 1.0, 0.0)
         for m in range(mem):
             value = jnp.sum(sums[m] * in_y, axis=0, keepdims=True)
             for c in range(sub):
                 part_send[to, c, m : m + 1, :] = value[:, c * chunk : (c + 1) * chunk]
-        for k in range(groups):
-            @pl.when(to * groups + k != me)
-            def _():
-                remote(
-                    part_send.at[to, k % sub], part_recv.at[me], part_send_sem, part_recv_sem, (k, to)
-                ).start()
-
-        return carry
-
-    lax.fori_loop(0, slabs, observe, 0)
+
+        def send(k):
+            which = k % sub if isinstance(k, int) else lax.rem(k, sub)
+            remote(
+                part_send.at[to, which], part_recv.at[me], part_send_sem, part_recv_sem, (k, to)
+            ).start()
+
+        each_peer(to, here, send)
+
+    each_slab(observe)
     part_recv[me] = part_send[s, own]
     drain(part_recv.at[pl.ds(0, total - 1)], part_recv_sem)
     if groups > 1:
@@ -284,15 +354,15 @@
         sums_send[r : r + 1, :] = jnp.sum(packed, axis=0, keepdims=True)
     sums_recv[me] = sums_send[...]
 
-    def spread(step, carry):
-        other = lax.rem(me + step, total)
-        remote(
-            sums_send, sums_recv.at[me], sums_send_sem, sums_recv_sem,
-            (lax.rem(other, groups), other // groups),
-        ).start()
-        return carry
-
-    lax.fori_loop(1, total, spread, 0)
+    def spread(to, here):
+        each_peer(
+            to, here,
+            lambda k: remote(
+                sums_send, sums_recv.at[me], sums_send_sem, sums_recv_sem, (k, to)
+            ).start(),
+        )
+
+    each_slab(spread)
     drain(sums_recv.at[pl.ds(0, total - 1)], sums_recv_sem)
     if total <= 64:
         whole = sums_recv[0]
@@ -320,7 +390,7 @@
             jnp.where(lane_m == members + g * mem + m, mixing, 0.0), axis=1, keepdims=True
         )
         column = jnp.broadcast_to(column, (members, coarse_x))
-        fresh = jnp.zeros(theta_ref.shape[1:], jnp.float32)
+        fresh = jnp.zeros(theta_new_ref.shape[1:], jnp.float32)
         for k in range(members):
             fresh = fresh + theta_all[k // mem, k % mem] * column[k : k + 1][None]
         theta_new_ref[m] = fresh
@@ -354,25 +424,31 @@
         functools.partial(kernel, groups, slabs, sub),
         name="window",
         out_shape=(
-            jax.ShapeDtypeStruct(state.shape, f32),
-            jax.ShapeDtypeStruct(theta.shape, f32),
+            pltpu.VMEM(state.shape, f32),
+            pltpu.VMEM(theta.shape, f32),
         ),
-        in_specs=[vmem] * 7,
+        in_specs=[pl.BlockSpec(memory_space=pl.ANY)] * 7,
         out_specs=(vmem, vmem),
         scratch_shapes=[
+            pltpu.VMEM(state.shape, f32),
+            pltpu.VMEM(forcing.shape, f32),
+            pltpu.VMEM(boxes.shape, boxes.dtype),
+            pltpu.VMEM((1, obs_slab), f32),
+            pltpu.VMEM((1, obs_slab), f32),
             pltpu.VMEM(state.shape, f32),
             pltpu.VMEM((mem, theta.shape[1], rows, cols), f32),
             pltpu.VMEM((2, 2, mem, rows, cols), f32),
             pltpu.VMEM((cols, obs_total), jnp.bfloat16),
             pltpu.VMEM((mem, planes, cols // LANES, rows, LANES), f32),
-            pltpu.VMEM((mem, planes, rows // TILE, cols), f32),
+            pltpu.VMEM((planes, mem, rows // TILE, cols), f32),
+            pltpu.VMEM((mem, rows // TILE, obs_total), f32),
             pltpu.VMEM((slabs, sub, mem, chunk), f32),
             pltpu.VMEM((total, mem, chunk), f32),
             pltpu.VMEM((groups, mem, chunk), f32),
             pltpu.VMEM((groups,) + theta.shape, f32),
             pltpu.VMEM((packs, LANES), f32),
             pltpu.VMEM((total, packs, LANES), f32),
-            dma((2, 2)), dma((2, 2)), dma, dma, dma, dma, dma, dma, dma, dma,
+            dma((7,)), dma((2, 2)), dma((2, 2)), dma, dma, dma, dma, dma, dma, dma, dma,
         ],
         compiler_params=pltpu.CompilerParams(collective_id=0, has_side_effects=True),
     )(state, theta, forcing, boxes, observed.reshape(1, -1), noise_var.reshape(1, -1), perturb)

time: 34.1 us -> 29.4 us (0.86)
  Pallas kernels: 30.8 us -> 27.1 us
  local copies, waits for them, and re-layouts: 2.55 us -> 1.42 us
    pallas_call x1, Pallas kernels: 30.8 us -> 27.1 us  [local(): pl.pallas_call(functools.partial(kernel, groups, slabs, sub), name='windo...]
    unnamed x4 -> x2, local copies, waits for them, and re-layouts: 2.55 us -> 1.42 us
where the time goes in v2:
time: 29.4 us; the launch traced here: 29.2 us
  Pallas kernels  27.1 us (92%)
  local copies, waits for them, and re-layouts  1.42 us (5%)
  between operations  0.64 us (2%)
    pallas_call x1, Pallas kernels, local(): pl.pallas_call(functools.partial(kernel, groups, slabs, sub), name='windo...  27.1 us
    unnamed x2, local copies, waits for them, and re-layouts  1.42 us

profile of v2, /device:TPU:0, one launch (start us, length us, event | category | flops | bytes accessed | tf_op | source)
XLA Modules:
  0.0 29.2 jit_solution(11510637340322768451)
XLA Ops:
  0.6 27.1 %window.1 = (f32[2,8,32,256]{3,2,1,0:T(8,128)S(1)}, f32[2,4,16,128]{3,2,1,0:T(8,128)S(1)}) custom-call(f32[2,8,32,256]{3,2,1,0:T(8,128)} %state_hbm.1, f32[2,4,16,128]{3,2,1,0:T(8,128)} %theta_hbm.1, f32[8,32,256]{2,1,0:T(8,128)} %forcing_hbm.1, s32[6,4096]{1,0:T(8,128)} %boxes_hbm.1, f32[1,512]{1,0:T(1,128)} %bitcast.2, f32[1,512]{1,0:T(1,128)} %bitcast.3, ...), custom_call_target="tpu_custom_call" | custom-call | tf_op jit(solution)/shard_map/window/pallas_call | solution.py:423
  27.8 0.8 %copy.11 = f32[2,8,32,256]{3,2,1,0:T(8,128)} copy(f32[2,8,32,256]{3,2,1,0:T(8,128)S(1)} %get-tuple-element.2) | data formatting | bytes 1048576
  28.6 0.6 %copy.12 = f32[2,4,16,128]{3,2,1,0:T(8,128)} copy(f32[2,4,16,128]{3,2,1,0:T(8,128)S(1)} %get-tuple-element.3) | data formatting | bytes 131072

commit v3 on v2

--- a/solution.py
+++ b/solution.py
@@ -206,7 +206,6 @@
             perturb_hbm.at[:, pl.ds(pl.multiple_of(want * chunk, LANES), chunk)],
             pert_all.at[g], pert_send_sem, pert_recv_sem, (other, s),
         ).start()
-        remote(theta_hbm, theta_all.at[g], theta_send_sem, theta_recv_sem, (other, s)).start()
 
     for load in loads[3:]:
         load.wait()
@@ -314,6 +313,10 @@
         each_peer(to, here, send)
 
     each_slab(observe)
+    for step in range(1, groups):
+        other = wrap(g + step, groups)
+        remote(theta_hbm, theta_all.at[g], theta_send_sem, theta_recv_sem, (other, s)).start()
+
     part_recv[me] = part_send[s, own]
     drain(part_recv.at[pl.ds(0, total - 1)], part_recv_sem)
     if groups > 1:
@@ -336,8 +339,6 @@
     anomaly = (predicted - jnp.mean(predicted, axis=0, keepdims=True)) / scale
     misfit = observed_ref[:, own_cols] + jnp.sqrt(noise) * perturbs - predicted
     weighted = anomaly / noise
-    if sub != groups:
-        weighted = weighted * (sub / groups)
 
     per_row = LANES // members
     packs = 2 * members // per_row
@@ -352,24 +353,24 @@
             value = jnp.sum(weighted * other, axis=1, keepdims=True)
             packed = packed + jnp.where(lane_m == slot * members + row_m, value, 0.0)
         sums_send[r : r + 1, :] = jnp.sum(packed, axis=0, keepdims=True)
-    sums_recv[me] = sums_send[...]
+    sums_recv[s] = sums_send[...]
 
     def spread(to, here):
-        each_peer(
-            to, here,
-            lambda k: remote(
-                sums_send, sums_recv.at[me], sums_send_sem, sums_recv_sem, (k, to)
-            ).start(),
-        )
+        def send():
+            remote(
+                sums_send, sums_recv.at[s], sums_send_sem, sums_recv_sem, (g, to)
+            ).start()
+
+        if here is None:
+            pl.when(to != s)(send)
+        elif not here:
+            send()
 
     each_slab(spread)
-    drain(sums_recv.at[pl.ds(0, total - 1)], sums_recv_sem)
-    if total <= 64:
-        whole = sums_recv[0]
-        for t in range(1, total):
-            whole = whole + sums_recv[t]
-    else:
-        whole = lax.fori_loop(1, total, lambda t, c: c + sums_recv[t], sums_recv[0])
+    drain(sums_recv.at[pl.ds(0, slabs - 1)], sums_recv_sem)
+    whole = sums_recv[0]
+    for t in range(1, slabs):
+        whole = whole + sums_recv[t]
 
     system = jnp.where(lane_m == row_m, 1.0, 0.0)
     for j in range(2 * members):
@@ -405,7 +406,7 @@
         drain(pert_all.at[pl.ds(0, groups - 1)], pert_send_sem)
         drain(theta_all.at[pl.ds(0, groups - 1)], theta_send_sem)
     drain(part_recv.at[pl.ds(0, total - 1)], part_send_sem)
-    drain(sums_recv.at[pl.ds(0, total - 1)], sums_send_sem)
+    drain(sums_recv.at[pl.ds(0, slabs - 1)], sums_send_sem)
 
 
 def local(groups, slabs, state, theta, forcing, boxes, observed, noise_var, perturb):
@@ -413,7 +414,7 @@
     total = groups * slabs
     obs_total = boxes.shape[1]
     obs_slab = obs_total // slabs
-    sub = min(groups, obs_slab // LANES)
+    sub = 1
     chunk = obs_slab // sub
     members = groups * mem
     packs = 2 * members * members // LANES
@@ -447,7 +448,7 @@
             pltpu.VMEM((groups, mem, chunk), f32),
             pltpu.VMEM((groups,) + theta.shape, f32),
             pltpu.VMEM((packs, LANES), f32),
-            pltpu.VMEM((total, packs, LANES), f32),
+            pltpu.VMEM((slabs, packs, LANES), f32),
             dma((7,)), dma((2, 2)), dma((2, 2)), dma, dma, dma, dma, dma, dma, dma, dma,
         ],
         compiler_params=pltpu.CompilerParams(collective_id=0, has_side_effects=True),

time: 29.4 us -> 28.7 us (0.976)
  Pallas kernels: 27.1 us -> 26.5 us
    pallas_call x1, Pallas kernels: 27.1 us -> 26.5 us  [local(): pl.pallas_call(functools.partial(kernel, groups, slabs, sub), name='windo...]
where the time goes in v3:
time: 28.7 us; the launch traced here: 28.5 us
  Pallas kernels  26.5 us (92%)
  local copies, waits for them, and re-layouts  1.42 us (5%)
  between operations  0.64 us (2%)
    pallas_call x1, Pallas kernels, local(): pl.pallas_call(functools.partial(kernel, groups, slabs, sub), name='windo...  26.5 us
    unnamed x2, local copies, waits for them, and re-layouts  1.42 us

profile of v3, /device:TPU:0, one launch (start us, length us, event | category | flops | bytes accessed | tf_op | source)
XLA Modules:
  0.0 28.5 jit_solution(15486975964570452851)
XLA Ops:
  0.6 26.5 %window.1 = (f32[2,8,32,256]{3,2,1,0:T(8,128)S(1)}, f32[2,4,16,128]{3,2,1,0:T(8,128)S(1)}) custom-call(f32[2,8,32,256]{3,2,1,0:T(8,128)} %state_hbm.1, f32[2,4,16,128]{3,2,1,0:T(8,128)} %theta_hbm.1, f32[8,32,256]{2,1,0:T(8,128)} %forcing_hbm.1, s32[6,4096]{1,0:T(8,128)} %boxes_hbm.1, f32[1,512]{1,0:T(1,128)} %bitcast.2, f32[1,512]{1,0:T(1,128)} %bitcast.3, ...), custom_call_target="tpu_custom_call" | custom-call | tf_op jit(solution)/shard_map/window/pallas_call | solution.py:424
  27.1 0.8 %copy.11 = f32[2,8,32,256]{3,2,1,0:T(8,128)} copy(f32[2,8,32,256]{3,2,1,0:T(8,128)S(1)} %get-tuple-element.2) | data formatting | bytes 1048576
  27.9 0.6 %copy.12 = f32[2,4,16,128]{3,2,1,0:T(8,128)} copy(f32[2,4,16,128]{3,2,1,0:T(8,128)S(1)} %get-tuple-element.3) | data formatting | bytes 131072

commit v4 on v3

--- a/solution.py
+++ b/solution.py
@@ -340,19 +340,15 @@
     misfit = observed_ref[:, own_cols] + jnp.sqrt(noise) * perturbs - predicted
     weighted = anomaly / noise
 
-    per_row = LANES // members
-    packs = 2 * members // per_row
     small = (members, LANES)
     lane_m = lax.broadcasted_iota(jnp.int32, small, 1)
     row_m = lax.broadcasted_iota(jnp.int32, small, 0)
-    for r in range(packs):
-        packed = jnp.zeros(small, jnp.float32)
-        for slot in range(per_row):
-            j = r * per_row + slot
-            other = anomaly[j : j + 1] if j < members else misfit[j - members : j - members + 1]
-            value = jnp.sum(weighted * other, axis=1, keepdims=True)
-            packed = packed + jnp.where(lane_m == slot * members + row_m, value, 0.0)
-        sums_send[r : r + 1, :] = jnp.sum(packed, axis=0, keepdims=True)
+    placed = jnp.zeros(small, jnp.float32)
+    for j in range(2 * members):
+        other = anomaly[j : j + 1] if j < members else misfit[j - members : j - members + 1]
+        value = jnp.sum(weighted * other, axis=1, keepdims=True)
+        placed = placed + jnp.where(lane_m == j, value, 0.0)
+    sums_send[...] = placed
     sums_recv[s] = sums_send[...]
 
     def spread(to, here):
@@ -372,13 +368,7 @@
     for t in range(1, slabs):
         whole = whole + sums_recv[t]
 
-    system = jnp.where(lane_m == row_m, 1.0, 0.0)
-    for j in range(2 * members):
-        r, slot = j // per_row, j % per_row
-        value = jnp.sum(
-            jnp.where(lane_m == slot * members + row_m, whole[r : r + 1], 0.0), axis=1, keepdims=True
-        )
-        system = system + jnp.where(lane_m == j, value, 0.0)
+    system = whole + jnp.where(lane_m == row_m, 1.0, 0.0)
     for k in range(members):
         pivot = system[k : k + 1] / system[k : k + 1, k : k + 1]
         system = jnp.where(row_m == k, pivot, system - system[:, k : k + 1] * pivot)
@@ -417,7 +407,6 @@
     sub = 1
     chunk = obs_slab // sub
     members = groups * mem
-    packs = 2 * members * members // LANES
     f32 = jnp.float32
     vmem = pl.BlockSpec(memory_space=pltpu.VMEM)
     dma = pltpu.SemaphoreType.DMA
@@ -447,8 +436,8 @@
             pltpu.VMEM((total, mem, chunk), f32),
             pltpu.VMEM((groups, mem, chunk), f32),
             pltpu.VMEM((groups,) + theta.shape, f32),
-            pltpu.VMEM((packs, LANES), f32),
-            pltpu.VMEM((slabs, packs, LANES), f32),
+            pltpu.VMEM((members, LANES), f32),
+            pltpu.VMEM((slabs, members, LANES), f32),
             dma((7,)), dma((2, 2)), dma((2, 2)), dma, dma, dma, dma, dma, dma, dma, dma,
         ],
         compiler_params=pltpu.CompilerParams(collective_id=0, has_side_effects=True),

time: 28.7 us -> 28.8 us (level)
  no operation moved by 1% of the time
where the time goes in v4:
time: 28.8 us; the launch traced here: 28.6 us
  Pallas kernels  26.6 us (92%)
  local copies, waits for them, and re-layouts  1.42 us (5%)
  between operations  0.64 us (2%)
    pallas_call x1, Pallas kernels, local(): pl.pallas_call(functools.partial(kernel, groups, slabs, sub), name='windo...  26.6 us
    unnamed x2, local copies, waits for them, and re-layouts  1.42 us

profile of v4, /device:TPU:0, one launch (start us, length us, event | category | flops | bytes accessed | tf_op | source)
XLA Modules:
  0.0 28.6 jit_solution(15371414051730535711)
XLA Ops:
  0.6 26.6 %window.1 = (f32[2,8,32,256]{3,2,1,0:T(8,128)S(1)}, f32[2,4,16,128]{3,2,1,0:T(8,128)S(1)}) custom-call(f32[2,8,32,256]{3,2,1,0:T(8,128)} %state_hbm.1, f32[2,4,16,128]{3,2,1,0:T(8,128)} %theta_hbm.1, f32[8,32,256]{2,1,0:T(8,128)} %forcing_hbm.1, s32[6,4096]{1,0:T(8,128)} %boxes_hbm.1, f32[1,512]{1,0:T(1,128)} %bitcast.2, f32[1,512]{1,0:T(1,128)} %bitcast.3, ...), custom_call_target="tpu_custom_call" | custom-call | tf_op jit(solution)/shard_map/window/pallas_call | solution.py:413
  27.2 0.8 %copy.11 = f32[2,8,32,256]{3,2,1,0:T(8,128)} copy(f32[2,8,32,256]{3,2,1,0:T(8,128)S(1)} %get-tuple-element.2) | data formatting | bytes 1048576
  28.0 0.6 %copy.12 = f32[2,4,16,128]{3,2,1,0:T(8,128)} copy(f32[2,4,16,128]{3,2,1,0:T(8,128)S(1)} %get-tuple-element.3) | data formatting | bytes 131072
